TPU v7x, 32 devices: a whole 2x2x4 slice. The times are simulated.
32 devices in a mesh: ctx: 8 (over z, x), fsdp: 4 (over y, core).
Axes of the slice: x: 2, y: 2, z: 4, core: 2. Of those that a mesh axis runs over, the one named last changes fastest.
Arguments:
- inputs: bfloat16 [2, 4, 4096, 512], P(None, 'fsdp', 'ctx'), may hold values from -6 to 6
- out_grad: bfloat16 [2, 4, 4096, 512], P(None, 'fsdp', 'ctx'), may hold values from -6 to 6
- segment_ids: int32 [2, 4, 4096], P(None, 'fsdp', 'ctx'), may hold values from 0 to 15, never falling along the last dimension, each value on 1 to 2048 neighbouring positions
- block_order: int32 [16], replicated, may hold values from 0 to 15, each once
- w_qkv: bfloat16 [512, 1536], P('fsdp'), may hold values from -0.25 to 0.25
- w_out: bfloat16 [512, 512], P('fsdp'), may hold values from -1 to 1
- w_up: bfloat16 [512, 2048], P('fsdp'), may hold values from -0.25 to 0.25
- w_down: bfloat16 [2048, 512], P('fsdp'), may hold values from -0.125 to 0.125
- norm1_gain: bfloat16 [512], P('fsdp'), may hold values from 0.25 to 1.75
- norm1_bias: bfloat16 [512], P('fsdp'), may hold values from -2 to 2
- norm2_gain: bfloat16 [512], P('fsdp'), may hold values from 0.25 to 1.75
- norm2_bias: bfloat16 [512], P('fsdp'), may hold values from -2 to 2
- out_bias: bfloat16 [512], P('fsdp'), may hold values from -2 to 2
- up_bias: bfloat16 [2048], P('fsdp'), may hold values from -3 to 3
- down_bias: bfloat16 [512], P('fsdp'), may hold values from -2 to 2
Outputs:
- outputs: bfloat16 [2, 4, 4096, 512], P(None, 'fsdp', 'ctx')
- input_grad: float32 [2, 4, 4096, 512], P(None, 'fsdp', 'ctx')
- grad_w_qkv: float32 [512, 1536], P('fsdp')
- grad_w_out: float32 [512, 512], P('fsdp')
- grad_w_up: float32 [512, 2048], P('fsdp')
- grad_w_down: float32 [2048, 512], P('fsdp')
- grad_norm1_gain: float32 [512], P('fsdp')
- grad_norm1_bias: float32 [512], P('fsdp')
- grad_norm2_gain: float32 [512], P('fsdp')
- grad_norm2_bias: float32 [512], P('fsdp')
- grad_out_bias: float32 [512], P('fsdp')
- grad_up_bias: float32 [2048], P('fsdp')
- grad_down_bias: float32 [512], P('fsdp')
Inputs may be any that keep to these rules, and one draw needn't show every extreme that they name: `segment_ids`: along each sequence's true positions document numbers start at 0 and never fall; each document has 1 to 2048 tokens and one has exactly 2048. `block_order`: each value appears exactly once.
All inputs are finite; a program needn't handle non-finite values.
Results may differ from a plain program's by a relative error of at most 0.02.
Values may be sent and summed in bfloat16 or wider, within the bound.
A program may use at most 256 MiB of HBM per device.

v0:
```python
import math
import jax
import jax.numpy as jnp
from jax import lax
from jax.sharding import PartitionSpec as P

H = 8
HD = 64
BLK = 256
norm_eps = 1e-05
mask_fill = -1e30


def layer_norm(values, gain_vec, offset):
    center = values - jnp.mean(values, axis=-1, keepdims=True)
    spread = jnp.mean(center * center, axis=-1, keepdims=True)
    return center * lax.rsqrt(spread + norm_eps) * gain_vec + offset


def gelu_exact(values):
    return 0.5 * values * (1.0 + lax.erf(values * (1.0 / math.sqrt(2.0))))


def score_block(query_heads, key_heads, query_doc, query_pos, key_doc, key_pos):
    raw_scores = jnp.einsum(
        "qhd,khd->hqk", query_heads, key_heads, preferred_element_type=jnp.float32
    ) * (1.0 / math.sqrt(HD))
    allowed = (query_doc[:, None] == key_doc[None, :]) & (key_pos[None, :] <= query_pos[:, None])
    return (raw_scores, allowed[None])


def soft_block(raw_scores, allowed, log_norm):
    return jnp.exp(jnp.where(allowed, raw_scores, mask_fill) - log_norm[:, :, None])


def row_log_norm(query_heads, key_blocks, doc_blocks, pos_blocks, query_doc, query_pos):

    def row_visit(running, block_item):
        row_top, row_sum = running
        key_heads, key_doc, key_pos = block_item
        raw_scores, allowed = score_block(
            query_heads, key_heads, query_doc, query_pos, key_doc, key_pos
        )
        masked = jnp.where(allowed, raw_scores, mask_fill)
        new_top = jnp.maximum(row_top, jnp.max(masked, axis=-1))
        fresh = jnp.sum(jnp.where(allowed, jnp.exp(masked - new_top[:, :, None]), 0.0), axis=-1)
        return ((new_top, row_sum * jnp.exp(row_top - new_top) + fresh), None)

    query_count = query_doc.shape[0]
    start = (
        jnp.full((H, query_count), mask_fill, jnp.float32),
        jnp.zeros((H, query_count), jnp.float32),
    )
    (row_top, row_sum), unused = lax.scan(row_visit, start, (key_blocks, doc_blocks, pos_blocks))
    return row_top + jnp.log(row_sum)


def attend(
    query_heads, key_blocks, value_blocks, doc_blocks, pos_blocks, query_doc, query_pos, log_norm
):

    def attend_visit(accum_out, block_item):
        key_heads, value_heads, key_doc, key_pos = block_item
        raw_scores, allowed = score_block(
            query_heads, key_heads, query_doc, query_pos, key_doc, key_pos
        )
        soft_low = soft_block(raw_scores, allowed, log_norm).astype(jnp.bfloat16)
        return (
            accum_out
            + jnp.einsum("hqk,khd->qhd", soft_low, value_heads, preferred_element_type=jnp.float32),
            None,
        )

    start = jnp.zeros(query_heads.shape, jnp.float32)
    accum_out, unused = lax.scan(
        attend_visit, start, (key_blocks, value_blocks, doc_blocks, pos_blocks)
    )
    return accum_out


def grad_block(
    query_heads,
    grad_heads,
    log_norm,
    row_delta,
    query_doc,
    query_pos,
    key_heads,
    value_heads,
    key_doc,
    key_pos,
):
    raw_scores, allowed = score_block(
        query_heads, key_heads, query_doc, query_pos, key_doc, key_pos
    )
    soft = soft_block(raw_scores, allowed, log_norm)
    grad_soft = jnp.einsum(
        "qhd,khd->hqk", grad_heads, value_heads, preferred_element_type=jnp.float32
    )
    grad_scores = (soft * (grad_soft - row_delta[:, :, None])).astype(jnp.bfloat16)
    score_scale = 1.0 / math.sqrt(HD)
    part_q = (
        jnp.einsum("hqk,khd->qhd", grad_scores, key_heads, preferred_element_type=jnp.float32)
        * score_scale
    )
    part_k = (
        jnp.einsum("hqk,qhd->khd", grad_scores, query_heads, preferred_element_type=jnp.float32)
        * score_scale
    )
    part_v = jnp.einsum(
        "hqk,qhd->khd", soft.astype(jnp.bfloat16), grad_heads, preferred_element_type=jnp.float32
    )
    return (part_q, part_k, part_v)


def body(
    inputs,
    out_grad,
    segment_ids,
    block_order,
    w_qkv,
    w_out,
    w_up,
    w_down,
    norm1_gain,
    norm1_bias,
    norm2_gain,
    norm2_bias,
    out_bias,
    up_bias,
    down_bias,
):
    gathered = (
        lax.all_gather(w_qkv, "fsdp", axis=0, tiled=True),
        lax.all_gather(w_out, "fsdp", axis=0, tiled=True),
        lax.all_gather(w_up, "fsdp", axis=0, tiled=True),
        lax.all_gather(w_down, "fsdp", axis=0, tiled=True),
        lax.all_gather(norm1_gain, "fsdp", axis=0, tiled=True),
        lax.all_gather(norm1_bias, "fsdp", axis=0, tiled=True),
        lax.all_gather(norm2_gain, "fsdp", axis=0, tiled=True),
        lax.all_gather(norm2_bias, "fsdp", axis=0, tiled=True),
        lax.all_gather(out_bias, "fsdp", axis=0, tiled=True),
        lax.all_gather(up_bias, "fsdp", axis=0, tiled=True),
        lax.all_gather(down_bias, "fsdp", axis=0, tiled=True),
    )
    full_qkv, full_out, full_up, full_down = (gathered[0], gathered[1], gathered[2], gathered[3])
    gain_one, bias_one, gain_two, bias_two, full_obias, full_ubias, full_dbias = [
        member.astype(jnp.float32) for member in gathered[4:]
    ]
    model_width = full_qkv.shape[0]
    local_rows = inputs.shape[2]
    ctx_count = lax.axis_size("ctx")
    seq_len = local_rows * ctx_count
    key_block = min(512, seq_len)
    block_count = seq_len // key_block
    ctx_index = lax.axis_index("ctx")
    row_ids = jnp.arange(local_rows, dtype=jnp.int32)
    own_blocks = lax.dynamic_slice_in_dim(block_order, 2 * ctx_index, 2)
    own_pos = own_blocks[row_ids // BLK] * BLK + row_ids % BLK
    all_ids = jnp.arange(seq_len, dtype=jnp.int32)
    all_pos = block_order[all_ids // BLK] * BLK + all_ids % BLK
    pos_blocks = all_pos.reshape(block_count, key_block)
    grad_sums = [jnp.zeros(member.shape, jnp.float32) for member in gathered]
    outputs_list = []
    input_grads = []
    for micro_idx in range(inputs.shape[0]):
        seq_in = inputs[micro_idx, 0].astype(jnp.float32)
        normed, norm1_pull = jax.vjp(layer_norm, seq_in, gain_one, bias_one)
        normed_low = normed.astype(jnp.bfloat16)
        qkv_out = jnp.dot(normed_low, full_qkv, preferred_element_type=jnp.float32).astype(
            jnp.bfloat16
        )
        query_heads = qkv_out[:, :model_width].reshape(local_rows, H, HD)
        kv_all, doc_all = (
            lax.all_gather(qkv_out[:, model_width:], "ctx", axis=0, tiled=True),
            lax.all_gather(segment_ids[micro_idx, 0], "ctx", axis=0, tiled=True),
        )
        doc_rows = doc_all[all_pos]
        query_doc = doc_all[own_pos]
        kv_heads = kv_all.reshape(block_count, key_block, 2, H, HD)
        key_blocks = kv_heads[:, :, 0]
        value_blocks = kv_heads[:, :, 1]
        doc_blocks = doc_rows.reshape(block_count, key_block)
        log_norm = row_log_norm(query_heads, key_blocks, doc_blocks, pos_blocks, query_doc, own_pos)
        attn_acc = attend(
            query_heads,
            key_blocks,
            value_blocks,
            doc_blocks,
            pos_blocks,
            query_doc,
            own_pos,
            log_norm,
        )
        attn_low = attn_acc.reshape(local_rows, model_width).astype(jnp.bfloat16)
        branch = jnp.dot(attn_low, full_out, preferred_element_type=jnp.float32) + full_obias
        middle = seq_in + branch
        normed_two, norm2_pull = jax.vjp(layer_norm, middle, gain_two, bias_two)
        normed_two_low = normed_two.astype(jnp.bfloat16)
        hidden = jnp.dot(normed_two_low, full_up, preferred_element_type=jnp.float32) + full_ubias
        active, gelu_pull = jax.vjp(gelu_exact, hidden)
        active_low = active.astype(jnp.bfloat16)
        result = middle + (
            jnp.dot(active_low, full_down, preferred_element_type=jnp.float32) + full_dbias
        )
        outputs_list.append(result.astype(jnp.bfloat16))
        grad_y = out_grad[micro_idx, 0]
        grad_y32 = grad_y.astype(jnp.float32)
        grad_sums[3] = grad_sums[3] + jnp.einsum(
            "rf,rd->fd", active_low, grad_y, preferred_element_type=jnp.float32
        )
        grad_sums[10] = grad_sums[10] + jnp.sum(grad_y32, axis=0)
        grad_active = jnp.einsum("rd,fd->rf", grad_y, full_down, preferred_element_type=jnp.float32)
        (grad_hidden,) = gelu_pull(grad_active)
        grad_hidden_low = grad_hidden.astype(jnp.bfloat16)
        grad_sums[2] = grad_sums[2] + jnp.einsum(
            "rd,rf->df", normed_two_low, grad_hidden_low, preferred_element_type=jnp.float32
        )
        grad_sums[9] = grad_sums[9] + jnp.sum(grad_hidden_low.astype(jnp.float32), axis=0)
        grad_normed_two = jnp.einsum(
            "rf,df->rd", grad_hidden_low, full_up, preferred_element_type=jnp.float32
        )
        grad_mid_ln, grad_gain_two, grad_bias_two = norm2_pull(grad_normed_two)
        grad_sums[6] = grad_sums[6] + grad_gain_two
        grad_sums[7] = grad_sums[7] + grad_bias_two
        grad_mid = grad_y32 + grad_mid_ln
        grad_mid_low = grad_mid.astype(jnp.bfloat16)
        grad_sums[1] = grad_sums[1] + jnp.einsum(
            "rd,re->de", attn_low, grad_mid_low, preferred_element_type=jnp.float32
        )
        grad_sums[8] = grad_sums[8] + jnp.sum(grad_mid_low.astype(jnp.float32), axis=0)
        grad_attn_low = jnp.einsum(
            "re,de->rd", grad_mid_low, full_out, preferred_element_type=jnp.float32
        ).astype(jnp.bfloat16)
        grad_heads = grad_attn_low.reshape(local_rows, H, HD)
        row_delta = jnp.sum(grad_heads.astype(jnp.float32) * attn_acc, axis=-1).T

        def back_visit(grad_query, block_item):
            key_heads, value_heads, key_doc, key_pos = block_item
            part_q, part_k, part_v = grad_block(
                query_heads,
                grad_heads,
                log_norm,
                row_delta,
                query_doc,
                own_pos,
                key_heads,
                value_heads,
                key_doc,
                key_pos,
            )
            joined = jnp.concatenate(
                [part_k.reshape(key_block, model_width), part_v.reshape(key_block, model_width)],
                axis=1,
            )
            return (grad_query + part_q, joined)

        grad_query, kv_terms = lax.scan(
            back_visit,
            jnp.zeros((local_rows, H, HD), jnp.float32),
            (key_blocks, value_blocks, doc_blocks, pos_blocks),
        )
        kv_grad = lax.psum_scatter(
            kv_terms.reshape(seq_len, 2 * model_width).astype(jnp.bfloat16),
            "ctx",
            scatter_dimension=0,
            tiled=True,
        ).astype(jnp.float32)
        grad_qkv_low = jnp.concatenate(
            [grad_query.reshape(local_rows, model_width), kv_grad], axis=1
        ).astype(jnp.bfloat16)
        grad_sums[0] = grad_sums[0] + jnp.einsum(
            "rd,re->de", normed_low, grad_qkv_low, preferred_element_type=jnp.float32
        )
        grad_normed = jnp.einsum(
            "re,de->rd", grad_qkv_low, full_qkv, preferred_element_type=jnp.float32
        )
        grad_in_ln, grad_gain_one, grad_bias_one = norm1_pull(grad_normed)
        grad_sums[4] = grad_sums[4] + grad_gain_one
        grad_sums[5] = grad_sums[5] + grad_bias_one
        input_grads.append(grad_mid + grad_in_ln)
    owned = (
        lax.psum_scatter(
            grad_sums[0].astype(jnp.bfloat16), "fsdp", scatter_dimension=0, tiled=True
        ).astype(jnp.float32),
        lax.psum_scatter(
            grad_sums[1].astype(jnp.bfloat16), "fsdp", scatter_dimension=0, tiled=True
        ).astype(jnp.float32),
        lax.psum_scatter(
            grad_sums[2].astype(jnp.bfloat16), "fsdp", scatter_dimension=0, tiled=True
        ).astype(jnp.float32),
        lax.psum_scatter(
            grad_sums[3].astype(jnp.bfloat16), "fsdp", scatter_dimension=0, tiled=True
        ).astype(jnp.float32),
        lax.psum_scatter(
            grad_sums[4].astype(jnp.bfloat16), "fsdp", scatter_dimension=0, tiled=True
        ).astype(jnp.float32),
        lax.psum_scatter(
            grad_sums[5].astype(jnp.bfloat16), "fsdp", scatter_dimension=0, tiled=True
        ).astype(jnp.float32),
        lax.psum_scatter(
            grad_sums[6].astype(jnp.bfloat16), "fsdp", scatter_dimension=0, tiled=True
        ).astype(jnp.float32),
        lax.psum_scatter(
            grad_sums[7].astype(jnp.bfloat16), "fsdp", scatter_dimension=0, tiled=True
        ).astype(jnp.float32),
        lax.psum_scatter(
            grad_sums[8].astype(jnp.bfloat16), "fsdp", scatter_dimension=0, tiled=True
        ).astype(jnp.float32),
        lax.psum_scatter(
            grad_sums[9].astype(jnp.bfloat16), "fsdp", scatter_dimension=0, tiled=True
        ).astype(jnp.float32),
        lax.psum_scatter(
            grad_sums[10].astype(jnp.bfloat16), "fsdp", scatter_dimension=0, tiled=True
        ).astype(jnp.float32),
    )
    summed = (
        lax.psum(owned[0].astype(jnp.bfloat16), "ctx").astype(jnp.float32),
        lax.psum(owned[1].astype(jnp.bfloat16), "ctx").astype(jnp.float32),
        lax.psum(owned[2].astype(jnp.bfloat16), "ctx").astype(jnp.float32),
        lax.psum(owned[3].astype(jnp.bfloat16), "ctx").astype(jnp.float32),
        lax.psum(owned[4].astype(jnp.bfloat16), "ctx").astype(jnp.float32),
        lax.psum(owned[5].astype(jnp.bfloat16), "ctx").astype(jnp.float32),
        lax.psum(owned[6].astype(jnp.bfloat16), "ctx").astype(jnp.float32),
        lax.psum(owned[7].astype(jnp.bfloat16), "ctx").astype(jnp.float32),
        lax.psum(owned[8].astype(jnp.bfloat16), "ctx").astype(jnp.float32),
        lax.psum(owned[9].astype(jnp.bfloat16), "ctx").astype(jnp.float32),
        lax.psum(owned[10].astype(jnp.bfloat16), "ctx").astype(jnp.float32),
    )
    return (
        jnp.stack(outputs_list)[:, None],
        jnp.stack(input_grads)[:, None],
        summed[0],
        summed[1],
        summed[2],
        summed[3],
        summed[4],
        summed[5],
        summed[6],
        summed[7],
        summed[8],
        summed[9],
        summed[10],
    )


def solution(mesh):
    return jax.shard_map(
        body,
        mesh=mesh,
        in_specs=(
            P(None, "fsdp", "ctx", None),
            P(None, "fsdp", "ctx", None),
            P(None, "fsdp", "ctx"),
            P(),
            P("fsdp", None),
            P("fsdp", None),
            P("fsdp", None),
            P("fsdp", None),
            P("fsdp"),
            P("fsdp"),
            P("fsdp"),
            P("fsdp"),
            P("fsdp"),
            P("fsdp"),
            P("fsdp"),
        ),
        out_specs=(
            P(None, "fsdp", "ctx", None),
            P(None, "fsdp", "ctx", None),
            P("fsdp", None),
            P("fsdp", None),
            P("fsdp", None),
            P("fsdp", None),
            P("fsdp"),
            P("fsdp"),
            P("fsdp"),
            P("fsdp"),
            P("fsdp"),
            P("fsdp"),
            P("fsdp"),
        ),
        check_vma=False,
    )
```

profile of v0, /device:TPU:0, one launch (start us, length us, event | category | flops | bytes accessed | tf_op | source)
XLA Modules:
  0.0 1195.3 jit_solution(4293471570105327463)
XLA Ops:
  21.4 10.5 all-gather.15.cloned.1.call-done
  45.4 27.0 %all-gather = s32[1,1,4096]{2,1,0:T(1,128)S(1)} all-gather(s32[1,1,512]{2,1,0:T(1,128)S(1)} %get-tuple-element.1148), channel_id=2, replica_groups=mesh['ctx'=8,'fsdp'=4] {'ctx'}, dimensions={2}, use_global_device_ids=true | all-gather | bytes 18432 | tf_op jit(solution)/shard_map/all_gather | solution.py:176
  85.7 23.0 %gather_fusion.1 = s32[4096]{0:T(1024)S(1)} fusion(s32[4096]{0:T(1024)S(1)} %bitcast.527, s32[4096]{0:T(1024)S(1)} %broadcast_clamp_fusion), kind=kCustom, calls=%fused_computation.1 | custom fusion | bytes 49152 | tf_op jit(solution)/shard_map/gather | solution.py:178
  108.7 26.7 %all-gather.1 = s32[1,1,4096]{2,1,0:T(1,128)S(1)} all-gather(s32[1,1,512]{2,1,0:T(1,128)S(1)} %get-tuple-element.1149), channel_id=3, replica_groups=mesh['ctx'=8,'fsdp'=4] {'ctx'}, dimensions={2}, use_global_device_ids=true | all-gather | bytes 18432 | tf_op jit(solution)/shard_map/all_gather | solution.py:176
  138.6 23.0 %gather_fusion.3 = s32[4096]{0:T(1024)S(1)} fusion(s32[4096]{0:T(1024)S(1)} %bitcast.529, s32[4096]{0:T(1024)S(1)} %broadcast_clamp_fusion), kind=kCustom, calls=%fused_computation.3 | custom fusion | bytes 49152 | tf_op jit(solution)/shard_map/gather | solution.py:178
  182.3 7.2 all_gather.50
  195.1 11.4 copy.162
  206.6 12.2 %copy.239 = bf16[128,8,8,512]{3,2,1,0:T(8,128)(2,1)} copy(bf16[128,8,8,512]{3,1,2,0:T(8,128)(2,1)} %bitcast.538) | data formatting | bytes 16777216
  227.5 50.1 %while.76 = (s32[]{:T(128)}, f32[8,512]{1,0:T(8,128)S(1)}, f32[8,512]{1,0:T(8,128)S(1)}, s32[512]{0:T(512)S(1)}, s32[8,512]{1,0:T(8,128)S(1)}, /*index=5*/s32[8,...) while((s32[]{:T(128)}, f32[8,512]{1,0:T(8,128)S(1)}, ...), condition=%wide.region_15.16_spmd.clone, body=%wide.region_12.15_spmd.clone.sunk | while | flops 286030336 | bytes 18847896 | solution.py:54
  277.6 10.2 all-gather.17.cloned.1.call-done
  287.8 11.7 copy.155
  299.6 12.2 %copy.238 = bf16[128,8,8,512]{3,2,1,0:T(8,128)(2,1)} copy(bf16[128,8,8,512]{3,1,2,0:T(8,128)(2,1)} %bitcast.539) | data formatting | bytes 16777216
  320.5 50.5 %while.74 = (s32[]{:T(128)}, f32[8,512]{1,0:T(8,128)S(1)}, f32[8,512]{1,0:T(8,128)S(1)}, s32[512]{0:T(512)S(1)}, s32[8,512]{1,0:T(8,128)S(1)}, /*index=5*/s32[8,...) while((s32[]{:T(128)}, f32[8,512]{1,0:T(8,128)S(1)}, ...), condition=%wide.region_5.6_spmd.clone, body=%wide.region_2.5_spmd.clone.sunk | while | flops 286030336 | bytes 18847896 | solution.py:54
  377.3 46.4 %while.75 = (s32[]{:T(128)}, f32[512,8,64]{0,2,1:T(8,128)S(1)}, bf16[8,512,8,64]{1,3,2,0:T(8,128)(2,1)}, s32[512]{0:T(512)S(1)}, s32[8,512]{1,0:T(8,128)S(1)}, /...) while((s32[]{:T(128)}, f32[512,8,64]{0,2,1:T(8,128)S(1)}, ...), condition=%wide.region_7.8_spmd.clone, body=%wide.region_6.7_spmd.clone.sunk | while | flops 546580992 | bytes 4234906 | solution.py:75
  430.4 46.4 %while.77 = (s32[]{:T(128)}, f32[512,8,64]{0,2,1:T(8,128)S(1)}, bf16[8,512,8,64]{1,3,2,0:T(8,128)(2,1)}, s32[512]{0:T(512)S(1)}, s32[8,512]{1,0:T(8,128)S(1)}, /...) while((s32[]{:T(128)}, f32[512,8,64]{0,2,1:T(8,128)S(1)}, ...), condition=%wide.region_17.18_spmd.clone, body=%wide.region_16.17_spmd.clone.sunk | while | flops 546580992 | bytes 4234906 | solution.py:75
  525.5 138.9 %while.78 = (s32[]{:T(128)}, f32[512,8,64]{0,2,1:T(8,128)}, bf16[8,512,1024]{2,1,0:T(8,128)(2,1)}, bf16[8,512,8,64]{1,3,2,0:T(8,128)(2,1)}, s32[512]{0:T(512)S(1...) while((s32[]{:T(128)}, f32[512,8,64]{0,2,1:T(8,128)}, ...), condition=%wide.region_24.25_spmd.clone, body=%wide.region_23.24_spmd.clone.sunk | while | flops 1367353856 | bytes 51714240 | solution.py:258
  668.7 131.5 %while.79 = (s32[]{:T(128)}, f32[512,8,64]{0,2,1:T(8,128)}, bf16[8,512,1024]{2,1,0:T(8,128)(2,1)}, bf16[8,512,8,64]{1,3,2,0:T(8,128)(2,1)}, s32[512]{0:T(512)S(1...) while((s32[]{:T(128)}, f32[512,8,64]{0,2,1:T(8,128)}, ...), condition=%wide.region_32.33_spmd.clone, body=%wide.region_31.32_spmd.clone.sunk | while | flops 1367353856 | bytes 51714240 | solution.py:258
  834.8 129.0 %reduce-scatter.9.cloned.1.call-done = bf16[512,1024]{1,0:T(8,128)(2,1)} async-done(((bf16[4096,1024]{1,0:T(8,128)(2,1)}), bf16[512,1024]{1,0:T(8,128)(2,1)}) %reduce-scatter.9.cloned.1.call-update) | async-done | bytes 1048592 | tf_op jit(solution)/shard_map/reduce_scatter | solution.py:263
  987.0 34.2 %reduce-scatter.15.cloned.1.call-done = bf16[128,2048]{1,0:T(8,128)(2,1)} async-done(((bf16[512,2048]{1,0:T(8,128)(2,1)}), bf16[128,2048]{1,0:T(8,128)(2,1)}) %reduce-scatter.15.cloned.1.call-update) | async-done | bytes 524304 | tf_op jit(solution)/shard_map/reduce_scatter | solution.py:289
  1021.1 33.9 %reduce-scatter.17.cloned.1.call-done = bf16[512,512]{1,0:T(8,128)(2,1)} async-done(((bf16[2048,512]{1,0:T(8,128)(2,1)}), bf16[512,512]{1,0:T(8,128)(2,1)}) %reduce-scatter.17.cloned.1.call-update) | async-done | bytes 524304 | tf_op jit(solution)/shard_map/reduce_scatter | solution.py:292
  1055.0 31.5 %reduce-scatter.11.cloned.1.call-done = bf16[128,1536]{1,0:T(8,128)(2,1)} async-done(((bf16[512,1536]{1,0:T(8,128)(2,1)}), bf16[128,1536]{1,0:T(8,128)(2,1)}) %reduce-scatter.11.cloned.1.call-update) | async-done | bytes 393232 | tf_op jit(solution)/shard_map/reduce_scatter | solution.py:283
  1091.7 10.5 all-reduce.9
  1102.8 22.1 %all-reduce.7 = (bf16[128]{0:T(256)(128)(2,1)S(1)}, bf16[128]{0:T(256)(128)(2,1)S(1)}, bf16[128]{0:T(256)(128)(2,1)S(1)}, bf16[128]{0:T(256)(128)(2,1)S(1)}, bf1...) all-reduce(bf16[128]{0:T(256)(128)(2,1)S(1)} %dynamic-slice.1, ...), channel_id=1, replica_groups=mesh['ctx'=8,'fsdp'=4] {'ctx'}, use_global_device_ids=true, to_apply=%region_47.48 | all-reduce | flops 1280 | bytes 5120 | tf_op jit(solution)/shard_map/psum | solution.py:322
  1131.7 48.7 %all-reduce.12.cloned.1.call-done = (bf16[128,1536]{1,0:T(8,128)(2,1)}, bf16[128,512]{1,0:T(8,128)(2,1)}, bf16[128,2048]{1,0:T(8,128)(2,1)}, bf16[512,512]{1,0:T(8,128)(2,1)}) async-done(((bf16[128,1536]{1,0:T(8,128)(2,1)}, bf16[128,512]{1,0:T(8,128)(2,1)}, bf16[128,2048]{1,0:T(8,128)(2,1)}, bf16[512,512]{1,0:T(8,128)(2,1)}), (bf16[128,1536]{1,0:T(8,128)(2,1)}, bf16[128,512]{1,0:T(8,128)(2,1)}, ...) | async-done | bytes 1572880 | tf_op jit(solution)/shard_map/psum | solution.py:318
  (807 shorter events, 689.0 us)
Async XLA Ops:
  7.2 24.8 %all-gather.15.cloned.1.call-start = ((), (), s32[]{:S(2)}) async-start(), calls=%async_computation.6 | async-start | bytes 1966080 | tf_op jit(solution)/shard_map/all_gather | solution.py:134
  7.9 187.2 %all-gather.23.cloned.1.call-start = ((), (), s32[]{:S(2)}) async-start(), calls=%async_computation.10 | async-start | bytes 9437184 | tf_op jit(solution)/shard_map/all_gather | solution.py:175
  36.8 251.0 %all-gather.17.cloned.1.call-start = ((), (), s32[]{:S(2)}) async-start(), calls=%async_computation.7 | async-start | bytes 9437184 | tf_op jit(solution)/shard_map/all_gather | solution.py:175
  37.1 441.5 %copy-start.7 = (bf16[1,1,512,512]{2,3,1,0:T(8,128)(2,1)}, bf16[1,1,512,512]{2,3,1,0:T(8,128)(2,1)S(1)}, u32[]{:S(2)}) copy-start(bf16[1,1,512,512]{2,3,1,0:T(8,128)(2,1)S(1)} %copy.202) | copy-start | bytes 1572868
  40.9 440.4 %all-gather.19.cloned.1.call-start = ((), (), s32[]{:S(2)}) async-start(), calls=%async_computation.8 | async-start | bytes 2621440 | tf_op jit(solution)/shard_map/all_gather | solution.py:136
  41.5 444.9 %all-gather.21.cloned.1.call-start = ((), (), s32[]{:S(2)}) async-start(), calls=%async_computation.9 | async-start | bytes 2621440 | tf_op jit(solution)/shard_map/all_gather | solution.py:137
  42.1 788.4 %reduce-scatter.7.cloned.1.call-start = ((), (), s32[]{:S(2)}) async-start(), calls=%async_computation.11 | async-start | bytes 9437184 | tf_op jit(solution)/shard_map/reduce_scatter | solution.py:263
  138.6 50.9 %copy-start.28 = (bf16[2,1,512,512]{3,2,1,0:T(8,128)(2,1)S(1)}, bf16[2,1,512,512]{3,2,1,0:T(8,128)(2,1)}, u32[]{:S(2)}) copy-start(bf16[2,1,512,512]{3,2,1,0:T(8,128)(2,1)} %param.28) | copy-start | bytes 3145732
  167.0 349.0 %copy-start.47 = (f32[4,1,128]{2,1,0:T(1,128)}, f32[4,1,128]{2,1,0:T(1,128)S(1)}, u32[]{:S(2)}) copy-start(f32[4,1,128]{2,1,0:T(1,128)S(1)} %convert_element_type.307) | copy-start | bytes 6148
  172.0 325.7 %copy-start.53 = (f32[4,1,128]{2,1,0:T(1,128)}, f32[4,1,128]{2,1,0:T(1,128)S(1)}, u32[]{:S(2)}) copy-start(f32[4,1,128]{2,1,0:T(1,128)S(1)} %convert_element_type.308) | copy-start | bytes 6148
  189.5 289.0 %copy-start.9 = (bf16[512,512]{1,0:T(8,128)(2,1)}, bf16[512,512]{1,0:T(8,128)(2,1)S(1)}, u32[]{:S(2)}) copy-start(bf16[512,512]{1,0:T(8,128)(2,1)S(1)} %all_gather.50) | copy-start | bytes 1572868
  664.4 299.4 %reduce-scatter.9.cloned.1.call-start = ((), (), s32[]{:S(2)}) async-start(), calls=%async_computation.12 | async-start | bytes 9437184 | tf_op jit(solution)/shard_map/reduce_scatter | solution.py:263
  800.3 186.7 %reduce-scatter.13.cloned.1.call-start = ((), (), s32[]{:S(2)}) async-start(), calls=%async_computation.14 | async-start | bytes 655360 | tf_op jit(solution)/shard_map/reduce_scatter | solution.py:286
  803.2 218.0 %reduce-scatter.15.cloned.1.call-start = ((), (), s32[]{:S(2)}) async-start(), calls=%async_computation.15 | async-start | bytes 2621440 | tf_op jit(solution)/shard_map/reduce_scatter | solution.py:289
  809.2 245.8 %reduce-scatter.17.cloned.1.call-start = ((), (), s32[]{:S(2)}) async-start(), calls=%async_computation.16 | async-start | bytes 2621440 | tf_op jit(solution)/shard_map/reduce_scatter | solution.py:292
  815.1 271.4 %reduce-scatter.11.cloned.1.call-start = ((), (), s32[]{:S(2)}) async-start(), calls=%async_computation.13 | async-start | bytes 1966080 | tf_op jit(solution)/shard_map/reduce_scatter | solution.py:283
  830.5 133.3 %copy-start.6 = (bf16[1,1,512,512]{2,3,1,0:T(8,128)(2,1)S(1)}, bf16[1,1,512,512]{2,3,1,0:T(8,128)(2,1)}, u32[]{:S(2)}) copy-start(bf16[1,1,512,512]{2,3,1,0:T(8,128)(2,1)} %copy-done.4) | copy-start | bytes 1572868
  830.5 133.3 %copy-start.62 = (f32[512]{0:T(512)S(1)}, f32[512]{0:T(512)}, u32[]{:S(2)}) copy-start(f32[512]{0:T(512)} %copy-done.61) | copy-start | bytes 6148
  830.5 133.3 %copy-start.68 = (f32[512]{0:T(512)S(1)}, f32[512]{0:T(512)}, u32[]{:S(2)}) copy-start(f32[512]{0:T(512)} %copy-done.67) | copy-start | bytes 6148
  968.2 212.2 %all-reduce.12.cloned.1.call-start = ((), (), s32[]{:S(2)}) async-start(), calls=%async_computation.17 | async-start | bytes 3145728 | tf_op jit(solution)/shard_map/psum | solution.py:318
  981.3 105.2 %copy-start.27 = (bf16[1,1,512,512]{2,3,1,0:T(8,128)(2,1)S(1)}, bf16[1,1,512,512]{2,3,1,0:T(8,128)(2,1)}, u32[]{:S(2)}) copy-start(bf16[1,1,512,512]{2,3,1,0:T(8,128)(2,1)} %copy.204) | copy-start | bytes 1572868
  981.3 105.2 %copy-start.78 = (f32[512]{0:T(512)S(1)}, f32[512]{0:T(512)}, u32[]{:S(2)}) copy-start(f32[512]{0:T(512)} %copy-done.77) | copy-start | bytes 6148
  986.3 103.6 %copy-start.23 = (bf16[1,1,512,512]{2,3,1,0:T(8,128)(2,1)S(1)}, bf16[1,1,512,512]{2,3,1,0:T(8,128)(2,1)}, u32[]{:S(2)}) copy-start(bf16[1,1,512,512]{2,3,1,0:T(8,128)(2,1)} %copy.205) | copy-start | bytes 1572868
  986.3 103.6 %copy-start.76 = (f32[512]{0:T(512)S(1)}, f32[512]{0:T(512)}, u32[]{:S(2)}) copy-start(f32[512]{0:T(512)} %copy-done.75) | copy-start | bytes 6148
  (88 other events, 731.3 us)
Sparse Core Ops, SparseCore 0:
  9.6 22.3 all-gather.14
  36.9 125.5 all-gather.22
  164.7 123.0 all-gather.16
  289.2 20.7 all-gather.18
  311.5 22.5 all-gather.20
  664.5 147.1 reduce-scatter.6
  815.8 147.9 reduce-scatter.8
  966.3 20.6 reduce-scatter.12
  989.7 31.4 reduce-scatter.14
  1023.5 31.4 reduce-scatter.16
  1058.3 28.1 reduce-scatter.10
  1090.2 90.2 all-reduce.11
where the time goes:
time: 1210 us; the launch traced here: 1200 us
  matrix products  395 us (33%)
  waiting for transfers between devices  301 us (25%)
  local copies, waits for them, and re-layouts  193 us (16%)
  other arithmetic  155 us (13%)
  blocking collectives  131 us (11%)
  between operations  17.2 us (1%)
    reduce_scatter x2, waiting for transfers between devices, body(): lax.psum_scatter(kv_terms.reshape(seq_len, 2 * model_width).astype(jnp.bf...  129 us
    dot_general x32, matrix products, score_block(): jnp.einsum('qhd,khd->hqk', query_heads, key_heads, preferred_element_type...  77.9 us
    dot_general x16, matrix products, attend_visit(): jnp.einsum('hqk,khd->qhd', soft_low, value_heads, preferred_element_type=...  66.4 us
    dot_general x16, matrix products, grad_block(): jnp.einsum('qhd,khd->hqk', grad_heads, value_heads, preferred_element_typ...  64.5 us
    mul x48, other arithmetic, body(): own_pos = own_blocks[row_ids // BLK] * BLK + row_ids % BLK  62.6 us
    unnamed x219, local copies, waits for them, and re-layouts  55.3 us
    all_gather x2, blocking collectives, body(): lax.all_gather(segment_ids[micro_idx, 0], 'ctx', axis=0, tiled=True)  53.6 us
    dot_general x16, matrix products, grad_block(): jnp.einsum('hqk,khd->qhd', grad_scores, key_heads, preferred_element_type...  50 us
  transfers between devices with their start and end apart: 12, of which 8 were waited for; matrix products, arithmetic and copies ran while one was open for 46% of the time, Pallas kernels for 0%

commit v1 on v0

--- a/solution.py
+++ b/solution.py
@@ -171,8 +171,33 @@
             jnp.bfloat16
         )
         query_heads = qkv_out[:, :model_width].reshape(local_rows, H, HD)
+
+        def shape_orders_on_mesh(mine, comm_axis):
+            arr_now = lax.axis_index(comm_axis)
+            y = lax.axis_size(comm_axis)
+            current_value, back, y_new = (y, arr_now, mine.shape[0])
+            reached = jnp.zeros(
+                [j * current_value if hop_no == 0 else j for hop_no, j in enumerate(mine.shape)],
+                mine.dtype,
+            )
+            k0 = 1
+            p_next = lax.dynamic_update_slice_in_dim(reached, mine, back * y_new, axis=0)
+            while k0 < current_value:
+                mine = lax.ppermute(
+                    mine,
+                    axis_name=comm_axis,
+                    perm=[
+                        (hop_no, (hop_no + 1) % current_value) for hop_no in range(current_value)
+                    ],
+                )
+                p_next = lax.dynamic_update_slice_in_dim(
+                    p_next, mine, (back - k0) % current_value * y_new, axis=0
+                )
+                k0 += 1
+            return p_next
+
         kv_all, doc_all = (
-            lax.all_gather(qkv_out[:, model_width:], "ctx", axis=0, tiled=True),
+            shape_orders_on_mesh(qkv_out[:, model_width:], "ctx"),
             lax.all_gather(segment_ids[micro_idx, 0], "ctx", axis=0, tiled=True),
         )
         doc_rows = doc_all[all_pos]

time: 1210 us -> 1700 us (1.40)
  matrix products: 395 us -> 582 us
  waiting for transfers between devices: 301 us -> 477 us
  other arithmetic: 155 us -> 195 us
  local copies, waits for them, and re-layouts: 193 us -> 229 us
  blocking collectives: 131 us -> 166 us
    ppermute x0 -> x14, waiting for transfers between devices: none -> 206 us  [shape_orders_on_mesh(): lax.ppermute(mine, axis_name=comm_axis, perm=[(hop_no, (hop_no + 1) % cur...]
    dot_general x32, matrix products: 77.9 us -> 130 us  [score_block(): jnp.einsum('qhd,khd->hqk', query_heads, key_heads, preferred_element_type...]
    dot_general x16, matrix products: 42.6 us -> 91.9 us  [grad_block(): jnp.einsum('hqk,qhd->khd', soft.astype(jnp.bfloat16), grad_heads, preferr...]
    dot_general x16, matrix products: 64.5 us -> 110 us  [grad_block(): jnp.einsum('qhd,khd->hqk', grad_heads, value_heads, preferred_element_typ...]
    reduce_sum x16, other arithmetic: 32.5 us -> 71.7 us  [row_visit(): jnp.sum(jnp.where(allowed, jnp.exp(masked - new_top[:, :, None]), 0.0), a...]
    all_gather x2, blocking collectives: 53.6 us -> 89.1 us  [body(): lax.all_gather(segment_ids[micro_idx, 0], 'ctx', axis=0, tiled=True)]
    ppermute x0 -> x14, local copies, waits for them, and re-layouts: none -> 26.4 us  [shape_orders_on_mesh(): lax.ppermute(mine, axis_name=comm_axis, perm=[(hop_no, (hop_no + 1) % cur...]
    dynamic_update_slice x0 -> x15, local copies, waits for them, and re-layouts: none -> 24.9 us  [the longest x13 23.7 us: shape_orders_on_mesh(): lax.dynamic_update_slice_in_dim(p_next, mine, (back - k0) % current_value...]
  transfers between devices with their start and end apart: 12 -> 24, of which waited for: 8 -> 16; matrix products, arithmetic and copies ran while one was open for 46% -> 45% of each run, Pallas kernels for 0% -> 0%
where the time goes in v1:
time: 1700 us; the launch traced here: 1680 us
  matrix products  582 us (34%)
  waiting for transfers between devices  477 us (28%)
  local copies, waits for them, and re-layouts  229 us (13%)
  other arithmetic  195 us (11%)
  blocking collectives  166 us (10%)
  between operations  17.8 us (1%)
    ppermute x14, waiting for transfers between devices, shape_orders_on_mesh(): lax.ppermute(mine, axis_name=comm_axis, perm=[(hop_no, (hop_no + 1) % cur...  206 us
    dot_general x32, matrix products, score_block(): jnp.einsum('qhd,khd->hqk', query_heads, key_heads, preferred_element_type...  130 us
    reduce_scatter x2, waiting for transfers between devices, body(): lax.psum_scatter(kv_terms.reshape(seq_len, 2 * model_width).astype(jnp.bf...  111 us
    dot_general x16, matrix products, grad_block(): jnp.einsum('qhd,khd->hqk', grad_heads, value_heads, preferred_element_typ...  110 us
    dot_general x16, matrix products, grad_block(): jnp.einsum('hqk,qhd->khd', soft.astype(jnp.bfloat16), grad_heads, preferr...  91.9 us
    all_gather x2, blocking collectives, body(): lax.all_gather(segment_ids[micro_idx, 0], 'ctx', axis=0, tiled=True)  89.1 us
    dot_general x16, matrix products, attend_visit(): jnp.einsum('hqk,khd->qhd', soft_low, value_heads, preferred_element_type=...  84.7 us
    reduce_sum x16, other arithmetic, row_visit(): jnp.sum(jnp.where(allowed, jnp.exp(masked - new_top[:, :, None]), 0.0), a...  71.7 us
  transfers between devices with their start and end apart: 24, of which 16 were waited for; matrix products, arithmetic and copies ran while one was open for 45% of the time, Pallas kernels for 0%

profile of v1, /device:TPU:0, one launch (start us, length us, event | category | flops | bytes accessed | tf_op | source)
XLA Modules:
  0.0 1683.2 jit_solution(3089020364499762147)
XLA Ops:
  39.3 24.3 %collective-permute-done.7 = bf16[512,1024]{1,0:T(8,128)(2,1)S(1)} collective-permute-done((bf16[512,1024]{1,0:T(8,128)(2,1)S(1)}, bf16[512,1024]{1,0:T(8,128)(2,1)S(1)}, u32[]{:S(2)}, u32[]{:S(2)}) %collective-permute-start.7) | collective-permute-done | bytes 1048608 | tf_op jit(solution)/shard_map/ppermute | solution.py:186
  63.6 22.5 %collective-permute-done = bf16[512,1024]{1,0:T(8,128)(2,1)S(1)} collective-permute-done((bf16[512,1024]{1,0:T(8,128)(2,1)S(1)}, bf16[512,1024]{1,0:T(8,128)(2,1)S(1)}, u32[]{:S(2)}, u32[]{:S(2)}) %collective-permute-start) | collective-permute-done | bytes 1048608 | tf_op jit(solution)/shard_map/ppermute | solution.py:186
  86.1 22.4 %collective-permute-done.8 = bf16[512,1024]{1,0:T(8,128)(2,1)S(1)} collective-permute-done((bf16[512,1024]{1,0:T(8,128)(2,1)S(1)}, bf16[512,1024]{1,0:T(8,128)(2,1)S(1)}, u32[]{:S(2)}, u32[]{:S(2)}) %collective-permute-start.8) | collective-permute-done | bytes 1048608 | tf_op jit(solution)/shard_map/ppermute | solution.py:186
  108.6 22.5 %collective-permute-done.1 = bf16[512,1024]{1,0:T(8,128)(2,1)S(1)} collective-permute-done((bf16[512,1024]{1,0:T(8,128)(2,1)S(1)}, bf16[512,1024]{1,0:T(8,128)(2,1)S(1)}, u32[]{:S(2)}, u32[]{:S(2)}) %collective-permute-start.1) | collective-permute-done | bytes 1048608 | tf_op jit(solution)/shard_map/ppermute | solution.py:186
  153.5 22.6 %collective-permute-done.2 = bf16[512,1024]{1,0:T(8,128)(2,1)} collective-permute-done((bf16[512,1024]{1,0:T(8,128)(2,1)S(1)}, bf16[512,1024]{1,0:T(8,128)(2,1)}, u32[]{:S(2)}, u32[]{:S(2)}) %collective-permute-start.2) | collective-permute-done | bytes 1048608 | tf_op jit(solution)/shard_map/ppermute | solution.py:186
  198.6 22.5 %collective-permute-done.3 = bf16[512,1024]{1,0:T(8,128)(2,1)} collective-permute-done((bf16[512,1024]{1,0:T(8,128)(2,1)}, bf16[512,1024]{1,0:T(8,128)(2,1)}, u32[]{:S(2)}, u32[]{:S(2)}) %collective-permute-start.3) | collective-permute-done | bytes 1048608 | tf_op jit(solution)/shard_map/ppermute | solution.py:186
  221.3 63.1 %all-gather.1 = s32[1,1,4096]{2,1,0:T(1,128)S(1)} all-gather(s32[1,1,512]{2,1,0:T(1,128)S(1)} %get-tuple-element.1149), channel_id=3, replica_groups=mesh['ctx'=8,'fsdp'=4] {'ctx'}, dimensions={2}, use_global_device_ids=true | all-gather | bytes 18432 | tf_op jit(solution)/shard_map/all_gather | solution.py:201
  289.5 23.0 %gather_fusion.3 = s32[4096]{0:T(1024)S(1)} fusion(s32[4096]{0:T(1024)S(1)} %bitcast.527, s32[4096]{0:T(1024)S(1)} %broadcast_clamp_fusion), kind=kCustom, calls=%fused_computation.3 | custom fusion | bytes 49152 | tf_op jit(solution)/shard_map/gather | solution.py:203
  312.5 26.0 %all-gather = s32[1,1,4096]{2,1,0:T(1,128)S(1)} all-gather(s32[1,1,512]{2,1,0:T(1,128)S(1)} %get-tuple-element.1148), channel_id=2, replica_groups=mesh['ctx'=8,'fsdp'=4] {'ctx'}, dimensions={2}, use_global_device_ids=true | all-gather | bytes 18432 | tf_op jit(solution)/shard_map/all_gather | solution.py:201
  341.7 23.0 %gather_fusion.1 = s32[4096]{0:T(1024)S(1)} fusion(s32[4096]{0:T(1024)S(1)} %bitcast.529, s32[4096]{0:T(1024)S(1)} %broadcast_clamp_fusion), kind=kCustom, calls=%fused_computation.1 | custom fusion | bytes 49152 | tf_op jit(solution)/shard_map/gather | solution.py:203
  428.2 18.6 %collective-permute-done.5 = bf16[512,1024]{1,0:T(8,128)(2,1)} collective-permute-done((bf16[512,1024]{1,0:T(8,128)(2,1)}, bf16[512,1024]{1,0:T(8,128)(2,1)}, u32[]{:S(2)}, u32[]{:S(2)}) %collective-permute-start.5) | collective-permute-done | bytes 1048608 | tf_op jit(solution)/shard_map/ppermute | solution.py:186
  473.6 17.6 %collective-permute-done.6 = bf16[512,1024]{1,0:T(8,128)(2,1)} collective-permute-done((bf16[512,1024]{1,0:T(8,128)(2,1)}, bf16[512,1024]{1,0:T(8,128)(2,1)}, u32[]{:S(2)}, u32[]{:S(2)}) %collective-permute-start.6) | collective-permute-done | bytes 1048608 | tf_op jit(solution)/shard_map/ppermute | solution.py:186
  519.3 104.3 %while.76 = (s32[]{:T(128)}, f32[8,512]{1,0:T(8,128)S(1)}, f32[8,512]{1,0:T(8,128)S(1)}, s32[512]{0:T(512)S(1)}, s32[8,512]{1,0:T(8,128)S(1)}, /*index=5*/s32[8,...) while((s32[]{:T(128)}, f32[8,512]{1,0:T(8,128)S(1)}, ...), condition=%wide.region_15.16_spmd.clone, body=%wide.region_12.15_spmd.clone.sunk | while | flops 286030336 | bytes 18847896 | solution.py:54
  623.6 55.4 %while.77 = (s32[]{:T(128)}, f32[512,8,64]{0,2,1:T(8,128)}, bf16[8,512,8,64]{1,3,2,0:T(8,128)(2,1)}, s32[512]{0:T(512)S(1)}, s32[8,512]{1,0:T(8,128)S(1)}, /*ind...) while((s32[]{:T(128)}, f32[512,8,64]{0,2,1:T(8,128)}, ...), condition=%wide.region_17.18_spmd.clone, body=%wide.region_16.17_spmd.clone.sunk | while | flops 546580992 | bytes 4234906 | solution.py:75
  702.6 95.8 %while.74 = (s32[]{:T(128)}, f32[8,512]{1,0:T(8,128)S(1)}, f32[8,512]{1,0:T(8,128)S(1)}, s32[512]{0:T(512)S(1)}, s32[8,512]{1,0:T(8,128)S(1)}, /*index=5*/s32[8,...) while((s32[]{:T(128)}, f32[8,512]{1,0:T(8,128)S(1)}, ...), condition=%wide.region_5.6_spmd.clone, body=%wide.region_2.5_spmd.clone.sunk | while | flops 286030336 | bytes 18847896 | solution.py:54
  798.5 55.4 %while.75 = (s32[]{:T(128)}, f32[512,8,64]{0,2,1:T(8,128)}, bf16[8,512,8,64]{1,3,2,0:T(8,128)(2,1)}, s32[512]{0:T(512)S(1)}, s32[8,512]{1,0:T(8,128)S(1)}, /*ind...) while((s32[]{:T(128)}, f32[512,8,64]{0,2,1:T(8,128)}, ...), condition=%wide.region_7.8_spmd.clone, body=%wide.region_6.7_spmd.clone.sunk | while | flops 546580992 | bytes 4234906 | solution.py:75
  904.7 194.4 %while.78 = (s32[]{:T(128)}, f32[512,8,64]{0,2,1:T(8,128)}, bf16[8,512,1024]{2,1,0:T(8,128)(2,1)}, bf16[8,512,8,64]{1,3,2,0:T(8,128)(2,1)}, s32[512]{0:T(512)S(1...) while((s32[]{:T(128)}, f32[512,8,64]{0,2,1:T(8,128)}, ...), condition=%wide.region_24.25_spmd.clone, body=%wide.region_23.24_spmd.clone.sunk | while | flops 1367353856 | bytes 102045944 | solution.py:283
  1107.6 198.7 %while.79 = (s32[]{:T(128)}, f32[512,8,64]{0,2,1:T(8,128)}, bf16[8,512,1024]{2,1,0:T(8,128)(2,1)}, bf16[8,512,8,64]{1,3,2,0:T(8,128)(2,1)}, s32[512]{0:T(512)S(1...) while((s32[]{:T(128)}, f32[512,8,64]{0,2,1:T(8,128)}, ...), condition=%wide.region_32.33_spmd.clone, body=%wide.region_31.32_spmd.clone.sunk | while | flops 1367353856 | bytes 102045944 | solution.py:283
  1341.5 110.5 %reduce-scatter.9.cloned.1.call-done = bf16[512,1024]{1,0:T(8,128)(2,1)} async-done(((bf16[4096,1024]{1,0:T(8,128)(2,1)}), bf16[512,1024]{1,0:T(8,128)(2,1)}) %reduce-scatter.9.cloned.1.call-update) | async-done | bytes 1048592 | tf_op jit(solution)/shard_map/reduce_scatter | solution.py:288
  1475.0 34.2 %reduce-scatter.15.cloned.1.call-done = bf16[128,2048]{1,0:T(8,128)(2,1)} async-done(((bf16[512,2048]{1,0:T(8,128)(2,1)}), bf16[128,2048]{1,0:T(8,128)(2,1)}) %reduce-scatter.15.cloned.1.call-update) | async-done | bytes 524304 | tf_op jit(solution)/shard_map/reduce_scatter | solution.py:314
  1509.2 34.0 %reduce-scatter.17.cloned.1.call-done = bf16[512,512]{1,0:T(8,128)(2,1)} async-done(((bf16[2048,512]{1,0:T(8,128)(2,1)}), bf16[512,512]{1,0:T(8,128)(2,1)}) %reduce-scatter.17.cloned.1.call-update) | async-done | bytes 524304 | tf_op jit(solution)/shard_map/reduce_scatter | solution.py:317
  1543.2 30.9 %reduce-scatter.11.cloned.1.call-done = bf16[128,1536]{1,0:T(8,128)(2,1)} async-done(((bf16[512,1536]{1,0:T(8,128)(2,1)}), bf16[128,1536]{1,0:T(8,128)(2,1)}) %reduce-scatter.11.cloned.1.call-update) | async-done | bytes 393232 | tf_op jit(solution)/shard_map/reduce_scatter | solution.py:308
  1591.6 21.9 %all-reduce.7 = (bf16[128]{0:T(256)(128)(2,1)S(1)}, bf16[128]{0:T(256)(128)(2,1)S(1)}, bf16[128]{0:T(256)(128)(2,1)S(1)}, bf16[128]{0:T(256)(128)(2,1)S(1)}, bf1...) all-reduce(bf16[128]{0:T(256)(128)(2,1)S(1)} %dynamic-slice.1, ...), channel_id=1, replica_groups=mesh['ctx'=8,'fsdp'=4] {'ctx'}, use_global_device_ids=true, to_apply=%region_47.48 | all-reduce | flops 1280 | bytes 5120 | tf_op jit(solution)/shard_map/psum | solution.py:347
  1617.1 51.0 %all-reduce.12.cloned.1.call-done = (bf16[128,1536]{1,0:T(8,128)(2,1)}, bf16[128,512]{1,0:T(8,128)(2,1)}, bf16[128,2048]{1,0:T(8,128)(2,1)}, bf16[512,512]{1,0:T(8,128)(2,1)}) async-done(((bf16[128,1536]{1,0:T(8,128)(2,1)}, bf16[128,512]{1,0:T(8,128)(2,1)}, bf16[128,2048]{1,0:T(8,128)(2,1)}, bf16[512,512]{1,0:T(8,128)(2,1)}), (bf16[128,1536]{1,0:T(8,128)(2,1)}, bf16[128,512]{1,0:T(8,128)(2,1)}, ...) | async-done | bytes 1572880 | tf_op jit(solution)/shard_map/psum | solution.py:343
  (942 shorter events, 1063.6 us)
Async XLA Ops:
  7.2 24.8 %all-gather.13.cloned.1.call-start = ((), (), s32[]{:S(2)}) async-start(), calls=%async_computation.6 | async-start | bytes 1966080 | tf_op jit(solution)/shard_map/all_gather | solution.py:134
  7.9 851.6 %all-gather.15.cloned.1.call-start = ((), (), s32[]{:S(2)}) async-start(), calls=%async_computation.7 | async-start | bytes 2621440 | tf_op jit(solution)/shard_map/all_gather | solution.py:136
  8.7 860.9 %all-gather.17.cloned.1.call-start = ((), (), s32[]{:S(2)}) async-start(), calls=%async_computation.8 | async-start | bytes 2621440 | tf_op jit(solution)/shard_map/all_gather | solution.py:137
  34.9 28.7 %collective-permute-start.7 = (bf16[512,1024]{1,0:T(8,128)(2,1)S(1)}, bf16[512,1024]{1,0:T(8,128)(2,1)S(1)}, u32[]{:S(2)}, u32[]{:S(2)}) collective-permute-start(bf16[512,1024]{1,0:T(8,128)(2,1)S(1)} %slice.88), channel_id=1, source_target_pairs={{0,4},{4,8},{8,12},{12,16},{16,20},{20,24},{24,28},{28,0},{1,5},{5... | collective-permute-start | bytes 3145736 | tf_op jit(solution)/shard_map/ppermute | solution.py:186
  37.7 48.4 %collective-permute-start = (bf16[512,1024]{1,0:T(8,128)(2,1)S(1)}, bf16[512,1024]{1,0:T(8,128)(2,1)S(1)}, u32[]{:S(2)}, u32[]{:S(2)}) collective-permute-start(bf16[512,1024]{1,0:T(8,128)(2,1)S(1)} %slice.84), channel_id=1, source_target_pairs={{0,4},{4,8},{8,12},{12,16},{16,20},{20,24},{24,28},{28,0},{1,5},{5... | collective-permute-start | bytes 3145736 | tf_op jit(solution)/shard_map/ppermute | solution.py:186
  63.6 44.9 %collective-permute-start.8 = (bf16[512,1024]{1,0:T(8,128)(2,1)S(1)}, bf16[512,1024]{1,0:T(8,128)(2,1)S(1)}, u32[]{:S(2)}, u32[]{:S(2)}) collective-permute-start(bf16[512,1024]{1,0:T(8,128)(2,1)S(1)} %collective-permute-done.7), channel_id=1, source_target_pairs={{0,4},{4,8},{8,12},{12,16},{16,20},{20,24},{24,28},{28,0},{1,5},{5... | collective-permute-start | bytes 3145736 | tf_op jit(solution)/shard_map/ppermute | solution.py:186
  86.1 44.9 %collective-permute-start.1 = (bf16[512,1024]{1,0:T(8,128)(2,1)S(1)}, bf16[512,1024]{1,0:T(8,128)(2,1)S(1)}, u32[]{:S(2)}, u32[]{:S(2)}) collective-permute-start(bf16[512,1024]{1,0:T(8,128)(2,1)S(1)} %collective-permute-done), channel_id=1, source_target_pairs={{0,4},{4,8},{8,12},{12,16},{16,20},{20,24},{24,28},{28,0},{1,5},{5... | collective-permute-start | bytes 3145736 | tf_op jit(solution)/shard_map/ppermute | solution.py:186
  108.6 44.9 %collective-permute-start.9 = (bf16[512,1024]{1,0:T(8,128)(2,1)S(1)}, bf16[512,1024]{1,0:T(8,128)(2,1)S(1)}, u32[]{:S(2)}, u32[]{:S(2)}) collective-permute-start(bf16[512,1024]{1,0:T(8,128)(2,1)S(1)} %collective-permute-done.8), channel_id=1, source_target_pairs={{0,4},{4,8},{8,12},{12,16},{16,20},{20,24},{24,28},{28,0},{1,5},{5... | collective-permute-start | bytes 3145736 | tf_op jit(solution)/shard_map/ppermute | solution.py:186
  131.0 45.0 %collective-permute-start.2 = (bf16[512,1024]{1,0:T(8,128)(2,1)S(1)}, bf16[512,1024]{1,0:T(8,128)(2,1)}, u32[]{:S(2)}, u32[]{:S(2)}) collective-permute-start(bf16[512,1024]{1,0:T(8,128)(2,1)S(1)} %collective-permute-done.1), channel_id=1, source_target_pairs={{0,4},{4,8},{8,12},{12,16},{16,20},{20,24},{24,28},{28,0},{1,5},{5... | collective-permute-start | bytes 3145736 | tf_op jit(solution)/shard_map/ppermute | solution.py:186
  131.1 1206.3 %reduce-scatter.7.cloned.1.call-start = ((), (), s32[]{:S(2)}) async-start(), calls=%async_computation.9 | async-start | bytes 9437184 | tf_op jit(solution)/shard_map/reduce_scatter | solution.py:288
  153.5 45.0 %collective-permute-start.10 = (bf16[512,1024]{1,0:T(8,128)(2,1)S(1)}, bf16[512,1024]{1,0:T(8,128)(2,1)}, u32[]{:S(2)}, u32[]{:S(2)}) collective-permute-start(bf16[512,1024]{1,0:T(8,128)(2,1)S(1)} %collective-permute-done.9), channel_id=1, source_target_pairs={{0,4},{4,8},{8,12},{12,16},{16,20},{20,24},{24,28},{28,0},{1,5},{5... | collective-permute-start | bytes 3145736 | tf_op jit(solution)/shard_map/ppermute | solution.py:186
  176.1 44.9 %collective-permute-start.3 = (bf16[512,1024]{1,0:T(8,128)(2,1)}, bf16[512,1024]{1,0:T(8,128)(2,1)}, u32[]{:S(2)}, u32[]{:S(2)}) collective-permute-start(bf16[512,1024]{1,0:T(8,128)(2,1)} %collective-permute-done.2), channel_id=1, source_target_pairs={{0,4},{4,8},{8,12},{12,16},{16,20},{20,24},{24,28},{28,0},{1,5},{5... | collective-permute-start | bytes 3145736 | tf_op jit(solution)/shard_map/ppermute | solution.py:186
  198.6 196.7 %collective-permute-start.11 = (bf16[512,1024]{1,0:T(8,128)(2,1)}, bf16[512,1024]{1,0:T(8,128)(2,1)}, u32[]{:S(2)}, u32[]{:S(2)}) collective-permute-start(bf16[512,1024]{1,0:T(8,128)(2,1)} %collective-permute-done.10), channel_id=1, source_target_pairs={{0,4},{4,8},{8,12},{12,16},{16,20},{20,24},{24,28},{28,0},{1,5},{5... | collective-permute-start | bytes 3145736 | tf_op jit(solution)/shard_map/ppermute | solution.py:186
  221.0 174.3 %collective-permute-start.4 = (bf16[512,1024]{1,0:T(8,128)(2,1)}, bf16[512,1024]{1,0:T(8,128)(2,1)}, u32[]{:S(2)}, u32[]{:S(2)}) collective-permute-start(bf16[512,1024]{1,0:T(8,128)(2,1)} %collective-permute-done.3), channel_id=1, source_target_pairs={{0,4},{4,8},{8,12},{12,16},{16,20},{20,24},{24,28},{28,0},{1,5},{5... | collective-permute-start | bytes 3145736 | tf_op jit(solution)/shard_map/ppermute | solution.py:186
  395.3 32.8 %collective-permute-start.12 = (bf16[512,1024]{1,0:T(8,128)(2,1)}, bf16[512,1024]{1,0:T(8,128)(2,1)}, u32[]{:S(2)}, u32[]{:S(2)}) collective-permute-start(bf16[512,1024]{1,0:T(8,128)(2,1)} %collective-permute-done.11), channel_id=1, source_target_pairs={{0,4},{4,8},{8,12},{12,16},{16,20},{20,24},{24,28},{28,0},{1,5},{5... | collective-permute-start | bytes 3145736 | tf_op jit(solution)/shard_map/ppermute | solution.py:186
  395.3 51.5 %collective-permute-start.5 = (bf16[512,1024]{1,0:T(8,128)(2,1)}, bf16[512,1024]{1,0:T(8,128)(2,1)}, u32[]{:S(2)}, u32[]{:S(2)}) collective-permute-start(bf16[512,1024]{1,0:T(8,128)(2,1)} %collective-permute-done.4), channel_id=1, source_target_pairs={{0,4},{4,8},{8,12},{12,16},{16,20},{20,24},{24,28},{28,0},{1,5},{5... | collective-permute-start | bytes 3145736 | tf_op jit(solution)/shard_map/ppermute | solution.py:186
  428.1 44.0 %collective-permute-start.13 = (bf16[512,1024]{1,0:T(8,128)(2,1)}, bf16[512,1024]{1,0:T(8,128)(2,1)}, u32[]{:S(2)}, u32[]{:S(2)}) collective-permute-start(bf16[512,1024]{1,0:T(8,128)(2,1)} %collective-permute-done.12), channel_id=1, source_target_pairs={{0,4},{4,8},{8,12},{12,16},{16,20},{20,24},{24,28},{28,0},{1,5},{5... | collective-permute-start | bytes 3145736 | tf_op jit(solution)/shard_map/ppermute | solution.py:186
  446.8 44.4 %collective-permute-start.6 = (bf16[512,1024]{1,0:T(8,128)(2,1)}, bf16[512,1024]{1,0:T(8,128)(2,1)}, u32[]{:S(2)}, u32[]{:S(2)}) collective-permute-start(bf16[512,1024]{1,0:T(8,128)(2,1)} %collective-permute-done.5), channel_id=1, source_target_pairs={{0,4},{4,8},{8,12},{12,16},{16,20},{20,24},{24,28},{28,0},{1,5},{5... | collective-permute-start | bytes 3145736 | tf_op jit(solution)/shard_map/ppermute | solution.py:186
  1099.1 352.9 %reduce-scatter.9.cloned.1.call-start = ((), (), s32[]{:S(2)}) async-start(), calls=%async_computation.10 | async-start | bytes 9437184 | tf_op jit(solution)/shard_map/reduce_scatter | solution.py:288
  1306.4 168.6 %reduce-scatter.13.cloned.1.call-start = ((), (), s32[]{:S(2)}) async-start(), calls=%async_computation.12 | async-start | bytes 655360 | tf_op jit(solution)/shard_map/reduce_scatter | solution.py:311
  1309.3 199.9 %reduce-scatter.15.cloned.1.call-start = ((), (), s32[]{:S(2)}) async-start(), calls=%async_computation.13 | async-start | bytes 2621440 | tf_op jit(solution)/shard_map/reduce_scatter | solution.py:314
  1315.9 227.3 %reduce-scatter.17.cloned.1.call-start = ((), (), s32[]{:S(2)}) async-start(), calls=%async_computation.14 | async-start | bytes 2621440 | tf_op jit(solution)/shard_map/reduce_scatter | solution.py:317
  1322.0 252.1 %reduce-scatter.11.cloned.1.call-start = ((), (), s32[]{:S(2)}) async-start(), calls=%async_computation.11 | async-start | bytes 1966080 | tf_op jit(solution)/shard_map/reduce_scatter | solution.py:308
  1456.5 211.5 %all-reduce.12.cloned.1.call-start = ((), (), s32[]{:S(2)}) async-start(), calls=%async_computation.15 | async-start | bytes 3145728 | tf_op jit(solution)/shard_map/psum | solution.py:343
  (141 other events, 4143.7 us)
Sparse Core Ops, SparseCore 0:
  9.6 22.3 all-gather.12
  33.5 22.5 all-gather.14
  131.2 23.0 all-gather.16
  1099.3 145.2 reduce-scatter.6
  1306.5 145.5 reduce-scatter.8
  1454.4 20.6 reduce-scatter.12
  1477.7 31.4 reduce-scatter.14
  1511.7 31.4 reduce-scatter.16
  1545.9 28.1 reduce-scatter.10
  1577.8 90.2 all-reduce.11
